TPU v7x, 256 devices: a whole 4x4x8 slice. The times are simulated.
256 devices in a mesh: row: 32 (over x, y, core), col: 8 (over z).
Axes of the slice: x: 4, y: 4, z: 8, core: 2. Of those that a mesh axis runs over, the one named last changes fastest.
Arguments:
- a_matrix: float32 [2048, 2048], P('row', 'col'), may hold values from -0.9 to 0.9
- b_matrix: float32 [2048, 2048], P('row', 'col'), may hold values from -0.9 to 0.9
- a_panel: float32 [2048, 1024], P('row', 'col'), may hold values from -0.9 to 0.9
- b_panel: float32 [2048, 1024], P('row', 'col'), may hold values from -0.9 to 0.9
Outputs:
- triangle: float32 [1024, 1024], P('row', 'col')
- pencil_cross: float32 [2048, 2048], P('row', 'col')
All inputs are finite; a program needn't handle non-finite values.
Results may differ from a plain program's by a relative error of at most 0.0003.
Values sent between devices are 32-bit elements; how exact they have to be, the bound alone decides.
A program may use at most 64 MiB of HBM per device.

v0:
```python
import jax
import jax.numpy as jnp
from jax import lax
from jax.sharding import PartitionSpec as P

HIGHEST = lax.Precision.HIGHEST


def in_one_piece(arrays, axis, dim, along):
    widths = [a.shape[along] for a in arrays]
    both = jnp.concatenate(arrays, axis=along)
    whole = lax.all_gather(both, axis, axis=dim, tiled=True)
    return tuple(jnp.split(whole, [sum(widths[:k]) for k in range(1, len(widths))], axis=along))


def in_blocks(x, dim, count):
    lengths = x.shape
    blocks = x.reshape(*lengths[:dim], count, lengths[dim] // count, *lengths[dim + 1 :])
    return jnp.moveaxis(blocks, dim, 0)


def summed_on_arrival(x, axis, dim):
    blocks = in_blocks(x, dim, lax.axis_size(axis))
    arrived = lax.all_to_all(blocks, axis, split_axis=0, concat_axis=0, tiled=True)
    return arrived.sum(axis=0)


def from_everyone(x, axis):
    count = lax.axis_size(axis)
    return lax.all_to_all(jnp.broadcast_to(x[None], (count, *x.shape)), axis, 0, 0, tiled=True)


def joined_along(blocks, dim):
    blocks = jnp.moveaxis(blocks, 0, dim)
    lengths = blocks.shape
    return blocks.reshape(*lengths[:dim], lengths[dim] * lengths[dim + 1], *lengths[dim + 2 :])


def gather_directly(x, axis, dim):
    blocks = from_everyone(x, axis)
    return joined_along(blocks, dim)


def local(a_matrix, b_matrix, a_panel, b_panel):
    row_count = a_matrix.shape[0]
    panel_width = a_panel.shape[1]
    full_a, full_pa, full_pb = (
        lax.all_gather(a_matrix, "col", axis=1, tiled=True),
        *in_one_piece((a_panel, b_panel), "col", 1, 0),
    )
    stacked = jnp.concatenate([full_pb, -full_pa], 0)
    own_block = jnp.concatenate([b_panel, -a_panel], 0)
    partial_gram = jnp.dot(own_block.T, stacked, precision=HIGHEST)
    gram_part = summed_on_arrival(partial_gram, "row", 1)
    gram_rows = gather_directly(gram_part, "row", 1)
    gram_matrix = lax.all_gather(gram_rows, "col", axis=0, tiled=True)
    lower_factor = jnp.linalg.cholesky(gram_matrix)
    q_rows = jax.scipy.linalg.solve_triangular(lower_factor, stacked.T, lower=True).T
    upper_rows = q_rows[:row_count]
    lower_rows = q_rows[row_count:]
    row_index = lax.axis_index("row")
    col_index = lax.axis_index("col")
    tri_rows = gram_matrix.shape[0] // lax.axis_size("row")
    corner = lax.dynamic_slice(
        lower_factor, (col_index * panel_width, row_index * tri_rows), (panel_width, tri_rows)
    )
    triangle = corner.T
    partial_z = jnp.dot(lower_rows.T, b_matrix, precision=HIGHEST)
    z_part = summed_on_arrival(partial_z, "row", 0)
    z_columns = gather_directly(z_part, "row", 0)
    v_block = jnp.dot(upper_rows, z_columns, precision=HIGHEST)
    pencil_cross = summed_on_arrival(-jnp.dot(full_a.T, v_block, precision=HIGHEST), "row", 0)
    return (triangle, pencil_cross)


def solution(mesh):
    in_specs = (P("row", "col"), P("row", "col"), P("row", "col"), P("row", "col"))
    out_specs = (P("row", "col"), P("row", "col"))
    return jax.shard_map(local, mesh=mesh, in_specs=in_specs, out_specs=out_specs, check_vma=False)
```

profile of v0, /device:TPU:1, one launch (start us, length us, event | category | flops | bytes accessed | tf_op | source)
XLA Modules:
  0.0 574.5 jit_solution(9497342517812801916)
XLA Ops:
  8.8 23.7 %all_gather.9 = f32[128,1024]{1,0:T(8,128)S(1)} all-gather(f32[128,128]{1,0:T(8,128)S(1)} %pad_maximum_fusion.2), channel_id=1, replica_groups=mesh['row'=32,'col'=8] {'col'}, dimensions={1}, use_global_device_ids=true | all-gather | bytes 589824 | tf_op jit(solution)/shard_map/all_gather | solution.py:12
  34.3 25.4 %all_to_all.25 = f32[32,128,32]{1,2,0:T(8,128)S(1)} all-to-all(f32[32,128,32]{1,2,0:T(8,128)S(1)} %bitcast.125), channel_id=1, replica_groups=mesh['row'=32,'col'=8] {'row'}, dimensions={0} | all-to-all | bytes 1048576 | tf_op jit(solution)/shard_map/all_to_all | solution.py:24
  59.8 15.1 %all_to_all.26 = f32[32,128,32]{1,2,0:T(8,128)} all-to-all(f32[32,128,32]{1,2,0:T(8,128)S(1)} %broadcast_in_dim.6), channel_id=1, replica_groups=mesh['row'=32,'col'=8] {'row'}, dimensions={0} | all-to-all | bytes 1048576 | tf_op jit(solution)/shard_map/all_to_all | solution.py:30
  75.0 53.9 %all-gather.2.cloned.1.call-done = f32[1024,1024]{0,1:T(8,128)} async-done(((f32[128,1024]{0,1:T(8,128)}), f32[1024,1024]{0,1:T(8,128)}) %all-gather.2.cloned.1.call-update) | async-done | bytes 4194320 | tf_op jit(solution)/shard_map/all_gather | solution.py:56
  128.9 5.8 %copy.16 = f32[1024,1024]{1,0:T(8,128)} copy(f32[1024,1024]{0,1:T(8,128)} %all-gather.2.cloned.1.call-done) | data formatting | bytes 8388608 | tf_op jit(solution)/shard_map/all_gather | solution.py:56
  134.7 4.4 fusion
  141.0 11.7 %cholesky.223 = f32[128,128]{1,0:T(8,128)S(1)} custom-call(f32[128,128]{1,0:T(8,128)S(1)} %cholesky.580), custom_call_target="Cholesky" | custom-call | tf_op jit(solution)/shard_map/jit(cholesky)/cholesky | solution.py:57
  152.8 2.5 cholesky.255
  155.3 9.8 %custom-call.63 = f32[1,128,128]{1,2,0:T(8,128)S(1)} custom-call(f32[1,128,128]{2,1,0:T(8,128)S(1)} %get-tuple-element.74), custom_call_target="InvertDiagBlocksLowerTriangular" | custom-call | tf_op jit(solution)/shard_map/jit(cholesky)/cholesky | solution.py:57
  168.9 11.9 %cholesky.244 = f32[128,128]{1,0:T(8,128)S(1)} custom-call(f32[128,128]{1,0:T(8,128)S(1)} %cholesky.584), custom_call_target="Cholesky" | custom-call | tf_op jit(solution)/shard_map/jit(cholesky)/cholesky | solution.py:57
  182.3 9.8 %custom-call.64 = f32[1,128,128]{1,2,0:T(8,128)S(1)} custom-call(f32[1,128,128]{2,1,0:T(8,128)S(1)} %get-tuple-element.71), custom_call_target="InvertDiagBlocksLowerTriangular" | custom-call | tf_op jit(solution)/shard_map/jit(cholesky)/cholesky | solution.py:57
  195.4 11.7 %cholesky.468 = f32[128,128]{1,0:T(8,128)S(1)} custom-call(f32[128,128]{1,0:T(8,128)S(1)} %cholesky.589), custom_call_target="Cholesky" | custom-call | tf_op jit(solution)/shard_map/jit(cholesky)/cholesky | solution.py:57
  208.4 9.8 %custom-call.65 = f32[1,128,128]{1,2,0:T(8,128)S(1)} custom-call(f32[1,128,128]{2,1,0:T(8,128)S(1)} %get-tuple-element.68), custom_call_target="InvertDiagBlocksLowerTriangular" | custom-call | tf_op jit(solution)/shard_map/jit(cholesky)/cholesky | solution.py:57
  219.4 2.3 convolution_subtract_fusion.2
  221.8 11.9 %cholesky.487 = f32[128,128]{1,0:T(8,128)S(1)} custom-call(f32[128,128]{1,0:T(8,128)S(1)} %cholesky.594), custom_call_target="Cholesky" | custom-call | tf_op jit(solution)/shard_map/jit(cholesky)/cholesky | solution.py:57
  235.0 9.8 %custom-call.66 = f32[1,128,128]{1,2,0:T(8,128)S(1)} custom-call(f32[1,128,128]{2,1,0:T(8,128)S(1)} %get-tuple-element.65), custom_call_target="InvertDiagBlocksLowerTriangular" | custom-call | tf_op jit(solution)/shard_map/jit(cholesky)/cholesky | solution.py:57
  245.9 2.3 convolution_subtract_fusion.3
  248.3 11.7 %cholesky.506 = f32[128,128]{1,0:T(8,128)S(1)} custom-call(f32[128,128]{1,0:T(8,128)S(1)} %cholesky.599), custom_call_target="Cholesky" | custom-call | tf_op jit(solution)/shard_map/jit(cholesky)/cholesky | solution.py:57
  261.4 10.2 %custom-call.67 = f32[1,128,128]{1,2,0:T(8,128)S(1)} custom-call(f32[1,128,128]{2,1,0:T(8,128)S(1)} %get-tuple-element.62), custom_call_target="InvertDiagBlocksLowerTriangular" | custom-call | tf_op jit(solution)/shard_map/jit(cholesky)/cholesky | solution.py:57
  274.9 11.7 %cholesky.526 = f32[128,128]{1,0:T(8,128)S(1)} custom-call(f32[128,128]{1,0:T(8,128)S(1)} %cholesky.604), custom_call_target="Cholesky" | custom-call | tf_op jit(solution)/shard_map/jit(cholesky)/cholesky | solution.py:57
  287.9 9.8 %custom-call.68 = f32[1,128,128]{1,2,0:T(8,128)S(1)} custom-call(f32[1,128,128]{2,1,0:T(8,128)S(1)} %get-tuple-element.59), custom_call_target="InvertDiagBlocksLowerTriangular" | custom-call | tf_op jit(solution)/shard_map/jit(cholesky)/cholesky | solution.py:57
  300.7 11.8 %cholesky.546 = f32[128,128]{1,0:T(8,128)S(1)} custom-call(f32[128,128]{1,0:T(8,128)S(1)} %cholesky.609), custom_call_target="Cholesky" | custom-call | tf_op jit(solution)/shard_map/jit(cholesky)/cholesky | solution.py:57
  313.8 9.8 %custom-call.69 = f32[1,128,128]{1,2,0:T(8,128)S(1)} custom-call(f32[1,128,128]{2,1,0:T(8,128)S(1)} %get-tuple-element.56), custom_call_target="InvertDiagBlocksLowerTriangular" | custom-call | tf_op jit(solution)/shard_map/jit(cholesky)/cholesky | solution.py:57
  326.2 11.7 %cholesky.564 = f32[128,128]{1,0:T(8,128)S(1)} custom-call(f32[128,128]{1,0:T(8,128)S(1)} %convolution_subtract_fusion.11), custom_call_target="Cholesky" | custom-call | tf_op jit(solution)/shard_map/jit(cholesky)/cholesky | solution.py:57
  344.9 6.6 %fusion.1 = (f32[1024,1024]{1,0:T(8,128)}, f32[1024,1024]{1,0:T(8,128)}) fusion(f32[1024,1024]{1,0:T(8,128)} %get-tuple-element.54, pred[]{:T(512)S(6)} %cholesky.579), kind=kLoop, calls=%fused_computation.6 | loop fusion | flops 4194304 | bytes 12582913 | tf_op jit(solution)/shard_map/jit(_solve_triangular)/triangular_solve | solution.py:58
  351.6 23.2 %while.1 = (s32[]{:T(128)}, f32[1024,1024]{1,0:T(8,128)}, s32[8,2]{0,1:T(2,128)S(1)}, f32[8,128,128]{2,1,0:T(8,128)S(1)}, s32[]{:T(128)}) while((s32[]{:T(128)}, f32[1024,1024]{1,0:T(8,128)}, s32[8,2]{0,1:T(2,128)S(1)}, f32[8,128,128]{2,1,0:T(8,128)S(1)}, s32[]{:T(128)}) %tuple.64), condition=%wide.while_cond, body=%wide.while_body.sunk | while | flops 2 | bytes 131181 | solution.py:58
  374.8 78.8 %custom-call.70 = f32[8,128,128]{1,2,0:T(8,128)S(1)} custom-call(f32[8,128,128]{2,1,0:T(8,128)S(1)} %get-tuple-element.9), custom_call_target="InvertDiagBlocksLowerTriangular" | custom-call | tf_op jit(solution)/shard_map/jit(_solve_triangular)/triangular_solve | solution.py:58
  467.8 27.9 %all_to_all.27 = f32[32,32,256]{2,1,0:T(8,128)S(1)} all-to-all(f32[32,32,256]{2,1,0:T(8,128)S(1)} %bitcast.121), channel_id=1, replica_groups=mesh['row'=32,'col'=8] {'row'}, dimensions={0} | all-to-all | bytes 2097152 | tf_op jit(solution)/shard_map/all_to_all | solution.py:24
  496.9 3.9 all-to-all-start.3
  500.9 20.7 %all_gather.11 = f32[64,2048]{1,0:T(8,128)S(1)} all-gather(f32[64,256]{1,0:T(8,128)S(1)} %copy-done.2), channel_id=1, replica_groups=mesh['row'=32,'col'=8] {'col'}, dimensions={1}, use_global_device_ids=true | all-gather | bytes 589824 | tf_op jit(solution)/shard_map/all_gather | solution.py:48
  526.4 12.0 %all-to-all-start.4 = ((f32[32,64,256]{2,1,0:T(8,128)}), f32[32,64,256]{2,1,0:T(8,128)S(1)}, u32[]{:S(2)}, u32[]{:S(2)}) async-start(f32[32,64,256]{2,1,0:T(8,128)} %bitcast.119), calls=%async_computation.4 | async-start | bytes 4194304 | tf_op jit(solution)/shard_map/all_to_all | solution.py:24
  540.0 26.7 %all-to-all-done.4 = f32[32,64,256]{2,1,0:T(8,128)S(1)} async-done(((f32[32,64,256]{2,1,0:T(8,128)}), f32[32,64,256]{2,1,0:T(8,128)S(1)}, u32[]{:S(2)}, u32[]{:S(2)}) %all-to-all-start.4) | async-done | bytes 2097184 | tf_op jit(solution)/shard_map/all_to_all | solution.py:24
  (103 shorter events, 79.3 us)
Async XLA Ops:
  7.2 459.6 %copy-start = (f32[64,256]{1,0:T(8,128)S(1)}, f32[64,256]{1,0:T(8,128)}, u32[]{:S(2)}) copy-start(f32[64,256]{1,0:T(8,128)} %param.5) | copy-start | bytes 196612
  7.2 121.7 %all-gather.2.cloned.1.call-start = ((), (), s32[]{:S(2)}) async-start(), calls=%async_computation.5 | async-start | bytes 4718592 | tf_op jit(solution)/shard_map/all_gather | solution.py:56
  139.1 1.9 copy-start.1
  466.5 34.4 %copy-start.2 = (f32[64,256]{1,0:T(8,128)S(1)}, f32[64,256]{1,0:T(8,128)}, u32[]{:S(2)}) copy-start(f32[64,256]{1,0:T(8,128)} %param.4) | copy-start | bytes 196612
  496.9 24.7 %all-to-all-start.3 = ((f32[32,32,256]{2,1,0:T(8,128)}), f32[32,32,256]{2,1,0:T(8,128)S(1)}, u32[]{:S(2)}, u32[]{:S(2)}) async-start(f32[32,32,256]{2,1,0:T(8,128)} %broadcast_in_dim.7), calls=%async_computation.3 | async-start | bytes 2097152 | tf_op jit(solution)/shard_map/all_to_all | solution.py:30
  526.4 40.3 %all-to-all-start.4 = ((f32[32,64,256]{2,1,0:T(8,128)}), f32[32,64,256]{2,1,0:T(8,128)S(1)}, u32[]{:S(2)}, u32[]{:S(2)}) async-start(f32[32,64,256]{2,1,0:T(8,128)} %bitcast.119), calls=%async_computation.4 | async-start | bytes 4194304 | tf_op jit(solution)/shard_map/all_to_all | solution.py:24
Sparse Core Ops, SparseCore 0:
  75.0 53.8 all-gather.1
where the time goes:
time: 579 us; the launch traced here: 575 us
  other arithmetic  265 us (46%)
  blocking collectives  113 us (20%)
  waiting for transfers between devices  80.6 us (14%)
  matrix products  41.5 us (7%)
  local copies, waits for them, and re-layouts  39 us (7%)
  between operations  19.7 us (3%)
  starting transfers between devices  15.9 us (3%)
    another operation x30, other arithmetic, local(): lower_factor = jnp.linalg.cholesky(gram_matrix)  172 us
    another operation x3, other arithmetic, local(): jax.scipy.linalg.solve_triangular(lower_factor, stacked.T, lower=True)  85.4 us
    all_gather x1, waiting for transfers between devices, local(): gram_matrix = lax.all_gather(gram_rows, 'col', axis=0, tiled=True)  53.9 us
    all_to_all x2, blocking collectives, summed_on_arrival(): lax.all_to_all(blocks, axis, split_axis=0, concat_axis=0, tiled=True)  53.3 us
    all_to_all x1, waiting for transfers between devices, summed_on_arrival(): lax.all_to_all(blocks, axis, split_axis=0, concat_axis=0, tiled=True)  26.7 us
    all_gather x1, blocking collectives, in_one_piece(): whole = lax.all_gather(both, axis, axis=dim, tiled=True)  23.7 us
    another operation x24, local copies, waits for them, and re-layouts  23 us
    another operation x14, matrix products, local(): lower_factor = jnp.linalg.cholesky(gram_matrix)  22.7 us
  transfers between devices with their start and end apart: 3, of which 2 were waited for; matrix products, arithmetic and copies ran while one was open for 0% of the time, Pallas kernels for 0%

commit v1 on v0

--- a/solution.py
+++ b/solution.py
@@ -53,7 +53,9 @@
     partial_gram = jnp.dot(own_block.T, stacked, precision=HIGHEST)
     gram_part = summed_on_arrival(partial_gram, "row", 1)
     gram_rows = gather_directly(gram_part, "row", 1)
-    gram_matrix = lax.all_gather(gram_rows, "col", axis=0, tiled=True)
+    gram_matrix = jnp.concatenate(
+        lax.all_to_all(jnp.stack([gram_rows] * lax.axis_size("col")), "col", 0, 0), axis=0
+    )
     lower_factor = jnp.linalg.cholesky(gram_matrix)
     q_rows = jax.scipy.linalg.solve_triangular(lower_factor, stacked.T, lower=True).T
     upper_rows = q_rows[:row_count]

time: 579 us -> 612 us (1.057)
  waiting for transfers between devices: 80.6 us -> 123 us
  between operations: 19.7 us -> 6.34 us
  local copies, waits for them, and re-layouts: 39 us -> 47.7 us
  blocking collectives: 113 us -> 105 us
    all_to_all x0 -> x1, waiting for transfers between devices: none -> 96.6 us  [local(): lax.all_to_all(jnp.stack([gram_rows] * lax.axis_size('col')), 'col', 0, 0)]
    all_gather x1 -> x0, waiting for transfers between devices: 53.9 us -> none  [local(): gram_matrix = lax.all_gather(gram_rows, 'col', axis=0, tiled=True)]
    reshape x0 -> x2, local copies, waits for them, and re-layouts: none -> 10.5 us  [local(): jnp.concatenate(lax.all_to_all(jnp.stack([gram_rows] * lax.axis_size('col...]
    all_to_all x2, blocking collectives: 53.3 us -> 45.8 us  [summed_on_arrival(): lax.all_to_all(blocks, axis, split_axis=0, concat_axis=0, tiled=True)]
    another operation x24 -> x25, local copies, waits for them, and re-layouts: 23 us -> 25.3 us
where the time goes in v1:
time: 612 us; the launch traced here: 607 us
  other arithmetic  264 us (43%)
  waiting for transfers between devices  123 us (20%)
  blocking collectives  105 us (17%)
  local copies, waits for them, and re-layouts  47.7 us (8%)
  matrix products  39.6 us (6%)
  starting transfers between devices  20.9 us (3%)
  between operations  6.34 us (1%)
    another operation x30, other arithmetic, local(): lower_factor = jnp.linalg.cholesky(gram_matrix)  172 us
    all_to_all x1, waiting for transfers between devices, local(): lax.all_to_all(jnp.stack([gram_rows] * lax.axis_size('col')), 'col', 0, 0)  96.6 us
    another operation x3, other arithmetic, local(): jax.scipy.linalg.solve_triangular(lower_factor, stacked.T, lower=True)  85.4 us
    all_to_all x2, blocking collectives, summed_on_arrival(): lax.all_to_all(blocks, axis, split_axis=0, concat_axis=0, tiled=True)  45.8 us
    all_to_all x1, waiting for transfers between devices, summed_on_arrival(): lax.all_to_all(blocks, axis, split_axis=0, concat_axis=0, tiled=True)  26.7 us
    all_gather x1, blocking collectives, in_one_piece(): whole = lax.all_gather(both, axis, axis=dim, tiled=True)  23.7 us
    another operation x24, local copies, waits for them, and re-layouts  23 us
    another operation x14, matrix products, local(): lower_factor = jnp.linalg.cholesky(gram_matrix)  22.7 us
  transfers between devices with their start and end apart: 3, of which 2 were waited for; matrix products, arithmetic and copies ran while one was open for 0% of the time, Pallas kernels for 0%

profile of v1, /device:TPU:1, one launch (start us, length us, event | category | flops | bytes accessed | tf_op | source)
XLA Modules:
  0.0 607.0 jit_solution(16648122044439986812)
XLA Ops:
  3.2 23.7 %all_gather.6 = f32[128,1024]{0,1:T(8,128)S(1)} all-gather(f32[128,128]{0,1:T(8,128)S(1)} %pad_maximum_fusion.2), channel_id=1, replica_groups=mesh['row'=32,'col'=8] {'col'}, dimensions={1}, use_global_device_ids=true | all-gather | bytes 589824 | tf_op jit(solution)/shard_map/all_gather | solution.py:12
  28.6 25.4 %all_to_all.30 = f32[32,128,32]{1,2,0:T(8,128)S(1)} all-to-all(f32[32,128,32]{1,2,0:T(8,128)S(1)} %bitcast.133), channel_id=1, replica_groups=mesh['row'=32,'col'=8] {'row'}, dimensions={0} | all-to-all | bytes 1048576 | tf_op jit(solution)/shard_map/all_to_all | solution.py:24
  54.0 15.0 %all_to_all.31 = f32[32,128,32]{1,2,0:T(8,128)S(1)} all-to-all(f32[32,128,32]{1,2,0:T(8,128)S(1)} %broadcast_in_dim.6), channel_id=1, replica_groups=mesh['row'=32,'col'=8] {'row'}, dimensions={0} | all-to-all | bytes 1048576 | tf_op jit(solution)/shard_map/all_to_all | solution.py:30
  71.3 4.5 all-to-all-start.2
  76.1 96.6 %all-to-all-done.2 = f32[8,128,1024]{1,2,0:T(8,128)} async-done(((f32[8,128,1024]{1,2,0:T(8,128)}), f32[8,128,1024]{1,2,0:T(8,128)}, u32[]{:S(2)}, u32[]{:S(2)}) %all-to-all-start.2) | async-done | bytes 4194336 | tf_op jit(solution)/shard_map/all_to_all | solution.py:57
  172.7 4.7 copy_bitcast_fusion
  177.5 5.8 copy.30
  183.2 4.1 fusion
  189.3 11.7 %cholesky.223 = f32[128,128]{1,0:T(8,128)S(1)} custom-call(f32[128,128]{1,0:T(8,128)S(1)} %cholesky.580), custom_call_target="Cholesky" | custom-call | tf_op jit(solution)/shard_map/jit(cholesky)/cholesky | solution.py:59
  201.0 2.5 cholesky.255
  203.5 9.8 %custom-call.63 = f32[1,128,128]{1,2,0:T(8,128)S(1)} custom-call(f32[1,128,128]{2,1,0:T(8,128)S(1)} %get-tuple-element.76), custom_call_target="InvertDiagBlocksLowerTriangular" | custom-call | tf_op jit(solution)/shard_map/jit(cholesky)/cholesky | solution.py:59
  217.1 11.9 %cholesky.244 = f32[128,128]{1,0:T(8,128)S(1)} custom-call(f32[128,128]{1,0:T(8,128)S(1)} %cholesky.584), custom_call_target="Cholesky" | custom-call | tf_op jit(solution)/shard_map/jit(cholesky)/cholesky | solution.py:59
  230.5 9.8 %custom-call.64 = f32[1,128,128]{1,2,0:T(8,128)S(1)} custom-call(f32[1,128,128]{2,1,0:T(8,128)S(1)} %get-tuple-element.73), custom_call_target="InvertDiagBlocksLowerTriangular" | custom-call | tf_op jit(solution)/shard_map/jit(cholesky)/cholesky | solution.py:59
  243.6 11.7 %cholesky.468 = f32[128,128]{1,0:T(8,128)S(1)} custom-call(f32[128,128]{1,0:T(8,128)S(1)} %cholesky.589), custom_call_target="Cholesky" | custom-call | tf_op jit(solution)/shard_map/jit(cholesky)/cholesky | solution.py:59
  256.6 9.8 %custom-call.65 = f32[1,128,128]{1,2,0:T(8,128)S(1)} custom-call(f32[1,128,128]{2,1,0:T(8,128)S(1)} %get-tuple-element.70), custom_call_target="InvertDiagBlocksLowerTriangular" | custom-call | tf_op jit(solution)/shard_map/jit(cholesky)/cholesky | solution.py:59
  270.0 11.9 %cholesky.487 = f32[128,128]{1,0:T(8,128)S(1)} custom-call(f32[128,128]{1,0:T(8,128)S(1)} %cholesky.594), custom_call_target="Cholesky" | custom-call | tf_op jit(solution)/shard_map/jit(cholesky)/cholesky | solution.py:59
  283.2 9.8 %custom-call.66 = f32[1,128,128]{1,2,0:T(8,128)S(1)} custom-call(f32[1,128,128]{2,1,0:T(8,128)S(1)} %get-tuple-element.67), custom_call_target="InvertDiagBlocksLowerTriangular" | custom-call | tf_op jit(solution)/shard_map/jit(cholesky)/cholesky | solution.py:59
  296.5 11.7 %cholesky.506 = f32[128,128]{1,0:T(8,128)S(1)} custom-call(f32[128,128]{1,0:T(8,128)S(1)} %cholesky.599), custom_call_target="Cholesky" | custom-call | tf_op jit(solution)/shard_map/jit(cholesky)/cholesky | solution.py:59
  309.6 10.2 %custom-call.67 = f32[1,128,128]{1,2,0:T(8,128)S(1)} custom-call(f32[1,128,128]{2,1,0:T(8,128)S(1)} %get-tuple-element.64), custom_call_target="InvertDiagBlocksLowerTriangular" | custom-call | tf_op jit(solution)/shard_map/jit(cholesky)/cholesky | solution.py:59
  323.1 11.7 %cholesky.526 = f32[128,128]{1,0:T(8,128)S(1)} custom-call(f32[128,128]{1,0:T(8,128)S(1)} %cholesky.604), custom_call_target="Cholesky" | custom-call | tf_op jit(solution)/shard_map/jit(cholesky)/cholesky | solution.py:59
  336.1 9.8 %custom-call.68 = f32[1,128,128]{1,2,0:T(8,128)S(1)} custom-call(f32[1,128,128]{2,1,0:T(8,128)S(1)} %get-tuple-element.61), custom_call_target="InvertDiagBlocksLowerTriangular" | custom-call | tf_op jit(solution)/shard_map/jit(cholesky)/cholesky | solution.py:59
  348.9 11.8 %cholesky.546 = f32[128,128]{1,0:T(8,128)S(1)} custom-call(f32[128,128]{1,0:T(8,128)S(1)} %cholesky.609), custom_call_target="Cholesky" | custom-call | tf_op jit(solution)/shard_map/jit(cholesky)/cholesky | solution.py:59
  362.0 9.8 %custom-call.69 = f32[1,128,128]{1,2,0:T(8,128)S(1)} custom-call(f32[1,128,128]{2,1,0:T(8,128)S(1)} %get-tuple-element.58), custom_call_target="InvertDiagBlocksLowerTriangular" | custom-call | tf_op jit(solution)/shard_map/jit(cholesky)/cholesky | solution.py:59
  374.4 11.7 %cholesky.564 = f32[128,128]{1,0:T(8,128)S(1)} custom-call(f32[128,128]{1,0:T(8,128)S(1)} %convolution_subtract_fusion.11), custom_call_target="Cholesky" | custom-call | tf_op jit(solution)/shard_map/jit(cholesky)/cholesky | solution.py:59
  393.1 6.6 %fusion.1 = (f32[1024,1024]{1,0:T(8,128)}, f32[1024,1024]{1,0:T(8,128)}) fusion(f32[1024,1024]{1,0:T(8,128)} %get-tuple-element.56, pred[]{:T(512)S(6)} %cholesky.579), kind=kLoop, calls=%fused_computation.7 | loop fusion | flops 4194304 | bytes 12582913 | tf_op jit(solution)/shard_map/jit(_solve_triangular)/triangular_solve | solution.py:60
  399.8 23.2 %while.1 = (s32[]{:T(128)}, f32[1024,1024]{1,0:T(8,128)}, s32[8,2]{0,1:T(2,128)S(1)}, f32[8,128,128]{2,1,0:T(8,128)S(1)}, s32[]{:T(128)}) while((s32[]{:T(128)}, f32[1024,1024]{1,0:T(8,128)}, s32[8,2]{0,1:T(2,128)S(1)}, f32[8,128,128]{2,1,0:T(8,128)S(1)}, s32[]{:T(128)}) %tuple.65), condition=%wide.while_cond, body=%wide.while_body.sunk | while | flops 2 | bytes 131181 | solution.py:60
  423.0 78.8 %custom-call.70 = f32[8,128,128]{1,2,0:T(8,128)S(1)} custom-call(f32[8,128,128]{2,1,0:T(8,128)S(1)} %get-tuple-element.9), custom_call_target="InvertDiagBlocksLowerTriangular" | custom-call | tf_op jit(solution)/shard_map/jit(_solve_triangular)/triangular_solve | solution.py:60
  514.5 20.5 %all_to_all.32 = f32[32,32,256]{2,1,0:T(8,128)S(1)} all-to-all(f32[32,32,256]{2,1,0:T(8,128)S(1)} %bitcast.130), channel_id=1, replica_groups=mesh['row'=32,'col'=8] {'row'}, dimensions={0} | all-to-all | bytes 2097152 | tf_op jit(solution)/shard_map/all_to_all | solution.py:24
  536.2 3.9 all-to-all-start.4
  540.1 20.4 %all_gather.7 = f32[64,2048]{1,0:T(8,128)S(1)} all-gather(f32[64,256]{1,0:T(8,128)S(1)} %copy-done.2), channel_id=1, replica_groups=mesh['row'=32,'col'=8] {'col'}, dimensions={1}, use_global_device_ids=true | all-gather | bytes 589824 | tf_op jit(solution)/shard_map/all_gather | solution.py:48
  565.3 12.4 %all-to-all-start.5 = ((f32[32,64,256]{2,1,0:T(8,128)}), f32[32,64,256]{2,1,0:T(8,128)S(1)}, u32[]{:S(2)}, u32[]{:S(2)}) async-start(f32[32,64,256]{2,1,0:T(8,128)} %bitcast.128), calls=%async_computation.5 | async-start | bytes 4194304 | tf_op jit(solution)/shard_map/all_to_all | solution.py:24
  579.3 26.7 %all-to-all-done.5 = f32[32,64,256]{2,1,0:T(8,128)S(1)} async-done(((f32[32,64,256]{2,1,0:T(8,128)}), f32[32,64,256]{2,1,0:T(8,128)S(1)}, u32[]{:S(2)}, u32[]{:S(2)}) %all-to-all-start.5) | async-done | bytes 2097184 | tf_op jit(solution)/shard_map/all_to_all | solution.py:24
  (106 shorter events, 85.6 us)
Async XLA Ops:
  0.6 512.9 %copy-start = (f32[64,256]{1,0:T(8,128)S(1)}, f32[64,256]{1,0:T(8,128)}, u32[]{:S(2)}) copy-start(f32[64,256]{1,0:T(8,128)} %param.5) | copy-start | bytes 196612
  71.3 101.4 %all-to-all-start.2 = ((f32[8,128,1024]{1,2,0:T(8,128)}), f32[8,128,1024]{1,2,0:T(8,128)}, u32[]{:S(2)}, u32[]{:S(2)}) async-start(f32[8,128,1024]{1,2,0:T(8,128)} %stack.3), calls=%async_computation.2 | async-start | bytes 8388608 | tf_op jit(solution)/shard_map/all_to_all | solution.py:57
  187.3 1.9 copy-start.1
  513.2 26.9 %copy-start.2 = (f32[64,256]{1,0:T(8,128)S(1)}, f32[64,256]{1,0:T(8,128)}, u32[]{:S(2)}) copy-start(f32[64,256]{1,0:T(8,128)} %param.4) | copy-start | bytes 196612
  536.2 24.4 %all-to-all-start.4 = ((f32[32,32,256]{2,1,0:T(8,128)}), f32[32,32,256]{2,1,0:T(8,128)S(1)}, u32[]{:S(2)}, u32[]{:S(2)}) async-start(f32[32,32,256]{2,1,0:T(8,128)} %broadcast_in_dim.7), calls=%async_computation.4 | async-start | bytes 2097152 | tf_op jit(solution)/shard_map/all_to_all | solution.py:30
  565.3 40.8 %all-to-all-start.5 = ((f32[32,64,256]{2,1,0:T(8,128)}), f32[32,64,256]{2,1,0:T(8,128)S(1)}, u32[]{:S(2)}, u32[]{:S(2)}) async-start(f32[32,64,256]{2,1,0:T(8,128)} %bitcast.128), calls=%async_computation.5 | async-start | bytes 4194304 | tf_op jit(solution)/shard_map/all_to_all | solution.py:24
